TPU v7x, 128 devices: a whole 4x4x4 slice. The times are simulated.
128 devices in a mesh: tp: 4 (over y_lo, core), dp: 32 (over x, z, y_hi).
Axes of the slice: x: 4, y: 4 (y_hi: 2, y_lo: 2; y = y_hi * 2 + y_lo), z: 4, core: 2. Of those that a mesh axis runs over, the one named last changes fastest.
Arguments:
- teacher_query: bfloat16 [8192, 8192], P('dp', 'tp'), may hold values from -8 to 8
- student_hidden: bfloat16 [8192, 4096], P('dp', 'tp'), may hold values from -16 to 16
- query_weight: bfloat16 [4096, 4096], P('dp', 'tp'), may hold values from -0.039794922 to 0.039794922
Outputs:
- kl_rows: float32 [128, 2048], P(('tp', 'dp'))
- weight_grad: float32 [4096, 4096], P('dp', 'tp')
All inputs are finite; a program needn't handle non-finite values.
Results may differ from a plain program's by a relative error of at most 0.0029.
Values may be sent and summed in bfloat16 or wider, within the bound.
No kernel may reach another device: no remote copies, remote signals or barrier semaphores. Data moves between devices by JAX's collectives and lax.ppermute only.
A program may use at most 64 MiB of HBM per device.

v0:
```python
import jax
import jax.numpy as jnp
from jax import lax
from jax.sharding import PartitionSpec as P

RHEADS = 32
NSEQ = 2
SEQ = 4096


def from_everyone(value, axis):
    copies = jnp.broadcast_to(value, (lax.axis_size(axis), *value.shape))
    return lax.all_to_all(copies, axis, split_axis=0, concat_axis=0, tiled=True)


def laid_out(parts, dim):
    lengths = list(parts.shape[1:])
    lengths[dim] *= parts.shape[0]
    return jnp.moveaxis(parts, 0, dim).reshape(lengths)


def gather_directly(value, axis, dim):
    parts = from_everyone(value, axis)
    return laid_out(parts, dim)


def in_one_piece(arrays, axis, split_dim, concat_dim, along):
    ends, at = ([], 0)
    for a in arrays[:-1]:
        at += a.shape[along]
        ends.append(at)
    both = jnp.concatenate(arrays, axis=along)
    return tuple(
        jnp.split(
            lax.all_to_all(both, axis, split_axis=split_dim, concat_axis=concat_dim, tiled=True),
            ends,
            axis=along,
        )
    )


def spread_heads(queries, heads, copies):
    rows = queries.shape[0]
    width = queries.shape[1] // heads
    shaped = queries.reshape(rows, heads, 1, width)
    return jnp.broadcast_to(shaped, (rows, heads, copies, width)).reshape(
        rows, heads * copies, width
    )


def local(teacher_query, student_hidden, query_weight):
    heads_here = RHEADS // lax.axis_size("tp")
    copies = lax.axis_size("dp") // heads_here
    rows = teacher_query.shape[0]
    teacher_width = teacher_query.shape[1] // heads_here
    hidden_full = gather_directly(student_hidden, "tp", 1)
    teacher_send = spread_heads(teacher_query, heads_here, copies)
    projected = jnp.dot(
        hidden_full,
        lax.all_gather(query_weight, "dp", axis=0, tiled=True),
        preferred_element_type=jnp.float32,
    )
    student_query = projected.astype(jnp.bfloat16)
    student_width = student_query.shape[1] // heads_here
    student_send = spread_heads(student_query, heads_here, copies)
    teacher_all, student_all = in_one_piece((teacher_send, student_send), "dp", 1, 0, 2)
    total_rows = teacher_all.shape[0]
    teacher_all = teacher_all.reshape(total_rows, teacher_width)
    student_all = student_all.reshape(total_rows, student_width)
    teacher_scale = teacher_width ** (-0.5)
    student_scale = student_width ** (-0.5)
    query_rows = SEQ // copies
    first_row = lax.axis_index("dp") % copies * query_rows
    block = min(512, query_rows)
    blocks_each = query_rows // block

    def relation_step(step, carry):
        kl_store, grad_store = carry
        sequence = step // blocks_each
        offset = step % blocks_each * block
        base = sequence * SEQ
        start = base + first_row + offset
        teacher_keys = lax.dynamic_slice_in_dim(teacher_all, base, SEQ, 0)
        student_keys = lax.dynamic_slice_in_dim(student_all, base, SEQ, 0)
        teacher_rows = lax.dynamic_slice_in_dim(teacher_all, start, block, 0)
        student_rows = lax.dynamic_slice_in_dim(student_all, start, block, 0)
        teacher_scores = (
            lax.dot_general(
                teacher_rows,
                teacher_keys,
                (((1,), (1,)), ((), ())),
                preferred_element_type=jnp.float32,
            )
            * teacher_scale
        )
        student_scores = (
            lax.dot_general(
                student_rows,
                student_keys,
                (((1,), (1,)), ((), ())),
                preferred_element_type=jnp.float32,
            )
            * student_scale
        )
        teacher_log = jax.nn.log_softmax(teacher_scores, axis=-1)
        student_log = jax.nn.log_softmax(student_scores, axis=-1)
        teacher_prob = jnp.exp(teacher_log)
        divergence = jnp.sum(teacher_prob * (teacher_log - student_log), axis=-1)
        score_grad = (jnp.exp(student_log) - teacher_prob).astype(jnp.bfloat16)
        key_part = (
            lax.dot_general(
                score_grad,
                student_rows,
                (((0,), (0,)), ((), ())),
                preferred_element_type=jnp.float32,
            )
            * student_scale
        )
        row_part = (
            jnp.dot(score_grad, student_keys, preferred_element_type=jnp.float32) * student_scale
        )
        seq_grad = lax.dynamic_slice_in_dim(grad_store, base, SEQ, 0)
        grad_store = lax.dynamic_update_slice_in_dim(grad_store, seq_grad + key_part, base, 0)
        current = lax.dynamic_slice_in_dim(grad_store, start, block, 0)
        grad_store = lax.dynamic_update_slice_in_dim(grad_store, current + row_part, start, 0)
        kl_store = lax.dynamic_update_slice_in_dim(
            kl_store, divergence, sequence * query_rows + offset, 0
        )
        return (kl_store, grad_store)

    kl_init = jnp.zeros((NSEQ * query_rows,), jnp.float32)
    grad_init = jnp.zeros((total_rows, student_width), jnp.float32)
    kl_store, grad_store = lax.fori_loop(0, NSEQ * blocks_each, relation_step, (kl_init, grad_init))
    returned = lax.all_to_all(
        grad_store.reshape(heads_here * copies, rows, student_width),
        "dp",
        split_axis=0,
        concat_axis=2,
        tiled=True,
    )
    summed = jnp.sum(returned.reshape(rows, heads_here, copies, student_width), axis=2)
    query_grad = summed.reshape(rows, heads_here * student_width).astype(jnp.bfloat16)
    feature_block = lax.all_to_all(hidden_full, "dp", split_axis=1, concat_axis=0, tiled=True)
    weight_grad = lax.dot_general(
        feature_block,
        lax.all_gather(query_grad, "dp", axis=0, tiled=True),
        (((0,), (0,)), ((), ())),
        preferred_element_type=jnp.float32,
    )
    return (kl_store.reshape(1, NSEQ * query_rows), weight_grad)


def solution(mesh):
    placed = (P("dp", "tp"), P("dp", "tp"), P("dp", "tp"))
    return jax.shard_map(
        local,
        mesh=mesh,
        in_specs=placed,
        out_specs=(P(("tp", "dp"), None), P("dp", "tp")),
        check_vma=False,
    )
```

profile of v0, /device:TPU:1, one launch (start us, length us, event | category | flops | bytes accessed | tf_op | source)
XLA Modules:
  0.0 572.4 jit_solution(10103598577909109360)
XLA Ops:
  7.2 0.0 all-gather.3.cloned.1.call-start
  7.2 0.7 all-gather.3.cloned.1.call-update
  7.9 1.2 copy.19
  9.1 1.5 broadcast_in_dim.29
  10.7 5.0 all-to-all-start
  15.7 1.3 copy.28
  17.0 25.4 %all-to-all-done = bf16[4,256,1024]{1,2,0:T(8,128)(2,1)S(1)} async-done(((bf16[4,256,1024]{1,2,0:T(8,128)(2,1)}), bf16[4,256,1024]{1,2,0:T(8,128)(2,1)S(1)}, u32[]{:S(2)}, u32[]{:S(2)}) %all-to-all-start) | async-done | bytes 2097184 | tf_op jit(solution)/shard_map/all_to_all | solution.py:13
  42.4 77.6 %all-gather.3.cloned.1.call-done = bf16[4096,1024]{1,0:T(8,128)(2,1)} async-done(((bf16[128,1024]{1,0:T(8,128)(2,1)}), bf16[4096,1024]{1,0:T(8,128)(2,1)}) %all-gather.3.cloned.1.call-update) | async-done | bytes 8388624 | tf_op jit(solution)/shard_map/all_gather | solution.py:60
  120.0 5.7 %fusion.16 = bf16[32,8,8,128]{3,2,1,0:T(8,128)(2,1)S(1)} fusion(bf16[256,4096]{0,1:T(8,128)(2,1)S(1)} %bitcast.49, bf16[4096,1024]{1,0:T(8,128)(2,1)} %all-gather.3.cloned.1.call-done), kind=kOutput, calls=%fused_computation.32 | convolution fusion | flops 2147745792 | bytes 11010048 | tf_op jit(solution)/shard_map/dot_general | solution.py:58
  125.8 0.0 copy-done.1
  125.8 0.1 copy.29
  125.9 0.5 broadcast_in_dim.31
  126.4 0.5 broadcast_in_dim.28
  126.9 3.4 pad_maximum_fusion
  130.3 5.4 all-to-all-start.1
  135.7 0.2 all-gather.5.cloned.1.call-start
  135.9 97.5 %all-to-all-done.1 = bf16[256,32,384]{2,0,1:T(8,128)(2,1)} async-done(((bf16[256,32,384]{2,0,1:T(8,128)(2,1)}), bf16[256,32,384]{2,0,1:T(8,128)(2,1)}, u32[]{:S(2)}, u32[]{:S(2)}) %all-to-all-start.1) | async-done | bytes 6291488 | tf_op jit(solution)/shard_map/all_to_all | solution.py:35
  233.4 1.7 slice_bitcast_fusion.1
  235.1 4.5 slice_bitcast_fusion
  239.6 2.3 broadcast_in_dim.26
  242.0 87.4 %while.17 = (s32[]{:T(128)}, f32[2048]{0:T(1024)S(1)}, f32[8192,128]{1,0:T(8,128)}, s32[]{:T(128)}, bf16[8192,256]{1,0:T(8,128)(2,1)}, /*index=5*/bf16[8192,128]...) while((s32[]{:T(128)}, f32[2048]{0:T(1024)S(1)}, ...), condition=%wide.region_4.6_spmd, body=%wide.region_0.5_spmd.sunk | while | flops 2729571840 | bytes 89164272 | solution.py:133
  242.0 3.1 multiply_reduce_fusion.5
  245.0 1.5 exponential_reduce_fusion.5
  246.5 1.3 multiply_reduce_fusion.6
  247.9 1.5 exponential_reduce_fusion.4
  249.4 5.7 subtract_convert_fusion.2
  255.1 0.2 dynamic_update_slice.37
  255.3 5.6 fusion.33
  260.9 0.0 copy-done
  260.9 3.0 fusion.34
  263.8 3.1 multiply_reduce_fusion.5
  266.9 1.5 exponential_reduce_fusion.5
  268.4 1.3 multiply_reduce_fusion.6
  269.7 1.5 exponential_reduce_fusion.4
  271.2 5.7 subtract_convert_fusion.2
  276.9 0.2 dynamic_update_slice.37
  277.1 5.6 fusion.33
  282.7 2.9 fusion.34
  285.6 3.1 multiply_reduce_fusion.5
  288.7 1.5 exponential_reduce_fusion.5
  290.2 1.3 multiply_reduce_fusion.6
  291.6 1.5 exponential_reduce_fusion.4
  293.1 5.7 subtract_convert_fusion.2
  298.7 0.2 dynamic_update_slice.37
  298.9 5.6 fusion.33
  304.6 2.9 fusion.34
  307.5 3.1 multiply_reduce_fusion.5
  310.5 1.5 exponential_reduce_fusion.5
  312.1 1.3 multiply_reduce_fusion.6
  313.4 1.5 exponential_reduce_fusion.4
  314.9 5.7 subtract_convert_fusion.2
  320.6 0.2 dynamic_update_slice.37
  320.8 5.6 fusion.33
  326.4 2.9 fusion.34
  329.3 54.7 %all_to_all.57 = f32[32,256,128]{2,1,0:T(8,128)S(1)} all-to-all(f32[32,256,128]{2,1,0:T(8,128)} %bitcast.48), channel_id=1, replica_groups=mesh['tp'=4,'dp'=32] {'dp'}, dimensions={0} | all-to-all | bytes 8388608 | tf_op jit(solution)/shard_map/all_to_all | solution.py:134
  384.1 0.2 bitcast_reduce_fusion
  384.3 1.0 copy.21
  385.3 0.0 all-gather.5.cloned.1.call-update
  385.4 0.0 copy-done.2
  385.4 37.5 %all_to_all.58 = bf16[256,32,128]{0,2,1:T(8,128)(2,1)} all-to-all(bf16[256,32,128]{0,2,1:T(8,128)(2,1)S(1)} %bitcast.50), channel_id=1, replica_groups=mesh['tp'=4,'dp'=32] {'dp'}, dimensions={1} | all-to-all | bytes 4194304 | tf_op jit(solution)/shard_map/all_to_all | solution.py:143
  422.8 3.2 copy.22
  426.1 130.4 %all-gather.5.cloned.1.call-done = bf16[8192,1024]{0,1:T(8,128)(2,1)} async-done(((bf16[256,1024]{0,1:T(8,128)(2,1)}), bf16[8192,1024]{0,1:T(8,128)(2,1)}) %all-gather.5.cloned.1.call-update) | async-done | bytes 16777232 | tf_op jit(solution)/shard_map/all_gather | solution.py:146
  556.5 8.1 %convolution_bitcast_fusion = f32[128,1024]{0,1:T(8,128)S(1)} fusion(bf16[8192,1024]{0,1:T(8,128)(2,1)} %all-gather.5.cloned.1.call-done, bf16[8192,128]{1,0:T(8,128)(2,1)S(1)} %bitcast.56), kind=kOutput, calls=%fused_computation.33 | convolution fusion | flops 2147483648 | bytes 19398656 | tf_op jit(solution)/shard_map/dot_general | solution.py:144
  564.6 1.0 copy.23
  (20 shorter events, 0.1 us)
Async XLA Ops:
  7.2 112.8 %all-gather.3.cloned.1.call-start = ((), (), s32[]{:S(2)}) async-start(), calls=%async_computation.4 | async-start | bytes 8650752 | tf_op jit(solution)/shard_map/all_gather | solution.py:60
  10.7 31.7 %all-to-all-start = ((bf16[4,256,1024]{1,2,0:T(8,128)(2,1)}), bf16[4,256,1024]{1,2,0:T(8,128)(2,1)S(1)}, u32[]{:S(2)}, u32[]{:S(2)}) async-start(bf16[4,256,1024]{1,2,0:T(8,128)(2,1)} %broadcast_in_dim.29), calls=%async_computation | async-start | bytes 4194304 | tf_op jit(solution)/shard_map/all_to_all | solution.py:13
  42.4 83.4 %copy-start.1 = (bf16[4,256,1024]{1,2,0:T(8,128)(2,1)}, bf16[4,256,1024]{1,2,0:T(8,128)(2,1)S(1)}, u32[]{:S(2)}) copy-start(bf16[4,256,1024]{1,2,0:T(8,128)(2,1)S(1)} %all-to-all-done) | copy-start | bytes 6291460
  130.3 103.1 %all-to-all-start.1 = ((bf16[256,32,384]{2,0,1:T(8,128)(2,1)}), bf16[256,32,384]{2,0,1:T(8,128)(2,1)}, u32[]{:S(2)}, u32[]{:S(2)}) async-start(bf16[256,32,384]{2,0,1:T(8,128)(2,1)} %pad_maximum_fusion), calls=%async_computation.1 | async-start | bytes 12582912 | tf_op jit(solution)/shard_map/all_to_all | solution.py:35
  135.7 420.8 %all-gather.5.cloned.1.call-start = ((), (), s32[]{:S(2)}) async-start(), calls=%async_computation.5 | async-start | bytes 17301504 | tf_op jit(solution)/shard_map/all_gather | solution.py:146
  255.3 5.6 copy-start
  277.1 5.6 copy-start
  298.9 5.6 copy-start
  320.8 5.6 copy-start
  329.3 55.0 %copy-start.3 = (f32[2048]{0:T(1024)}, f32[2048]{0:T(1024)S(1)}, u32[]{:S(2)}) copy-start(f32[2048]{0:T(1024)S(1)} %get-tuple-element.161) | copy-start | bytes 24580
  329.3 56.0 %copy-start.2 = (bf16[4,256,1024]{1,2,0:T(8,128)(2,1)S(1)}, bf16[4,256,1024]{1,2,0:T(8,128)(2,1)}, u32[]{:S(2)}) copy-start(bf16[4,256,1024]{1,2,0:T(8,128)(2,1)} %copy-done.1) | copy-start | bytes 6291460
Sparse Core Ops, SparseCore 0:
  11.0 108.9 all-gather.2
  385.5 170.9 all-gather.4
where the time goes:
time: 573 us; the launch traced here: 572 us
  waiting for transfers between devices  332 us (58%)
  blocking collectives  92.2 us (16%)
  matrix products  65.7 us (11%)
  other arithmetic  38.4 us (7%)
  local copies, waits for them, and re-layouts  19.7 us (3%)
  between operations  14.2 us (2%)
  starting transfers between devices  10.6 us (2%)
    all_gather x1, waiting for transfers between devices, local(): lax.all_gather(query_grad, 'dp', axis=0, tiled=True)  130 us
    all_to_all x1, waiting for transfers between devices, in_one_piece(): lax.all_to_all(both, axis, split_axis=split_dim, concat_axis=concat_dim,...  97.5 us
    all_gather x1, waiting for transfers between devices, local(): lax.all_gather(query_weight, 'dp', axis=0, tiled=True)  77.6 us
    all_to_all x1, blocking collectives, local(): lax.all_to_all(grad_store.reshape(heads_here * copies, rows, student_widt...  54.7 us
    all_to_all x1, blocking collectives, local(): lax.all_to_all(hidden_full, 'dp', split_axis=1, concat_axis=0, tiled=True)  37.5 us
    all_to_all x1, waiting for transfers between devices, from_everyone(): return lax.all_to_all(copies, axis, split_axis=0, concat_axis=0, tiled=True)  25.4 us
    convert_element_type x4, other arithmetic, relation_step(): score_grad = (jnp.exp(student_log) - teacher_prob).astype(jnp.bfloat16)  22.7 us
    dot_general x4, matrix products, relation_step(): lax.dot_general(score_grad, student_rows, (((0,), (0,)), ((), ())), prefe...  22.5 us
  transfers between devices with their start and end apart: 4, of which 4 were waited for; matrix products, arithmetic and copies ran while one was open for 1% of the time, Pallas kernels for 0%

commit v1 on v0

--- a/solution.py
+++ b/solution.py
@@ -143,7 +143,9 @@
     feature_block = lax.all_to_all(hidden_full, "dp", split_axis=1, concat_axis=0, tiled=True)
     weight_grad = lax.dot_general(
         feature_block,
-        lax.all_gather(query_grad, "dp", axis=0, tiled=True),
+        jnp.concatenate(
+            lax.all_to_all(jnp.stack([query_grad] * lax.axis_size("dp")), "dp", 0, 0), axis=0
+        ),
         (((0,), (0,)), ((), ())),
         preferred_element_type=jnp.float32,
     )

time: 573 us -> 646 us (1.13); the launches traced: 572 us -> 634 us
  blocking collectives: 92.2 us -> 193 us
  waiting for transfers between devices: 332 us -> 278 us
  starting transfers between devices: 10.6 us -> 25.8 us
    all_gather x1 -> x0, waiting for transfers between devices: 130 us -> none  [local(): lax.all_gather(query_grad, 'dp', axis=0, tiled=True)]
    all_to_all x2 -> x1, blocking collectives: 92.2 us -> 193 us  [local(): lax.all_to_all(jnp.stack([query_grad] * lax.axis_size('dp')), 'dp', 0, 0)]
    all_to_all x0 -> x2, waiting for transfers between devices: none -> 75.6 us  [the longest x1 48.9 us: local(): lax.all_to_all(grad_store.reshape(heads_here * copies, rows, student_widt...]
    all_to_all x0 -> x2, starting transfers between devices: none -> 15.2 us  [the longest x1 10 us: local(): lax.all_to_all(hidden_full, 'dp', split_axis=1, concat_axis=0, tiled=True)]
  transfers between devices with their start and end apart: 4 -> 5, of which waited for: 4 -> 5; matrix products, arithmetic and copies ran while one was open for 1% -> 2% of each run, Pallas kernels for 0% -> 0%
where the time goes in v1:
time: 646 us; the launch traced here: 634 us
  waiting for transfers between devices  278 us (43%)
  blocking collectives  193 us (30%)
  matrix products  62 us (10%)
  other arithmetic  40.8 us (6%)
  starting transfers between devices  25.8 us (4%)
  local copies, waits for them, and re-layouts  20.5 us (3%)
  between operations  14.2 us (2%)
    all_to_all x1, blocking collectives, local(): lax.all_to_all(jnp.stack([query_grad] * lax.axis_size('dp')), 'dp', 0, 0)  193 us
    all_to_all x1, waiting for transfers between devices, in_one_piece(): lax.all_to_all(both, axis, split_axis=split_dim, concat_axis=concat_dim,...  98.4 us
    all_gather x1, waiting for transfers between devices, local(): lax.all_gather(query_weight, 'dp', axis=0, tiled=True)  77.7 us
    all_to_all x1, waiting for transfers between devices, local(): lax.all_to_all(grad_store.reshape(heads_here * copies, rows, student_widt...  48.9 us
    all_to_all x1, waiting for transfers between devices, local(): lax.all_to_all(hidden_full, 'dp', split_axis=1, concat_axis=0, tiled=True)  26.7 us
    all_to_all x1, waiting for transfers between devices, from_everyone(): return lax.all_to_all(copies, axis, split_axis=0, concat_axis=0, tiled=True)  25.4 us
    convert_element_type x4, other arithmetic, relation_step(): score_grad = (jnp.exp(student_log) - teacher_prob).astype(jnp.bfloat16)  22.6 us
    dot_general x4, matrix products, relation_step(): lax.dot_general(score_grad, student_rows, (((0,), (0,)), ((), ())), prefe...  22.4 us
  transfers between devices with their start and end apart: 5, of which 5 were waited for; matrix products, arithmetic and copies ran while one was open for 2% of the time, Pallas kernels for 0%

profile of v1, /device:TPU:1, one launch (start us, length us, event | category | flops | bytes accessed | tf_op | source)
XLA Modules:
  0.0 634.0 jit_solution(11472864168270042675)
XLA Ops:
  7.2 0.0 all-gather.2.cloned.1.call-start
  7.2 0.7 all-gather.2.cloned.1.call-update
  7.9 1.2 copy.19
  9.1 1.5 broadcast_in_dim.29
  10.7 5.0 all-to-all-start
  15.7 1.3 copy.28
  16.9 25.4 %all-to-all-done = bf16[4,256,1024]{1,2,0:T(8,128)(2,1)S(1)} async-done(((bf16[4,256,1024]{1,2,0:T(8,128)(2,1)}), bf16[4,256,1024]{1,2,0:T(8,128)(2,1)S(1)}, u32[]{:S(2)}, u32[]{:S(2)}) %all-to-all-start) | async-done | bytes 2097184 | tf_op jit(solution)/shard_map/all_to_all | solution.py:13
  42.4 77.7 %all-gather.2.cloned.1.call-done = bf16[4096,1024]{1,0:T(8,128)(2,1)} async-done(((bf16[128,1024]{1,0:T(8,128)(2,1)}), bf16[4096,1024]{1,0:T(8,128)(2,1)}) %all-gather.2.cloned.1.call-update) | async-done | bytes 8388624 | tf_op jit(solution)/shard_map/all_gather | solution.py:60
  120.0 5.7 fusion.18
  125.8 0.0 copy-done.1
  125.8 0.1 copy.29
  125.9 0.5 broadcast_in_dim.31
  126.4 0.5 broadcast_in_dim.28
  126.9 3.4 pad_maximum_fusion
  130.3 5.6 all-to-all-start.1
  135.9 98.4 %all-to-all-done.1 = bf16[256,32,384]{2,0,1:T(8,128)(2,1)} async-done(((bf16[256,32,384]{2,0,1:T(8,128)(2,1)}), bf16[256,32,384]{2,0,1:T(8,128)(2,1)}, u32[]{:S(2)}, u32[]{:S(2)}) %all-to-all-start.1) | async-done | bytes 6291488 | tf_op jit(solution)/shard_map/all_to_all | solution.py:35
  234.3 1.7 slice_bitcast_fusion.1
  236.0 4.5 slice_bitcast_fusion
  240.5 2.3 broadcast_in_dim.26
  242.8 87.3 %while.17 = (s32[]{:T(128)}, f32[2048]{0:T(1024)S(1)}, f32[8192,128]{1,0:T(8,128)}, s32[]{:T(128)}, bf16[8192,256]{1,0:T(8,128)(2,1)}, /*index=5*/bf16[8192,128]...) while((s32[]{:T(128)}, f32[2048]{0:T(1024)S(1)}, ...), condition=%wide.region_4.6_spmd, body=%wide.region_0.5_spmd.sunk | while | flops 2729571840 | bytes 89164272 | solution.py:133
  242.8 3.1 multiply_reduce_fusion.5
  245.9 1.5 exponential_reduce_fusion.5
  247.4 1.3 multiply_reduce_fusion.6
  248.8 1.5 exponential_reduce_fusion.4
  250.3 5.7 subtract_convert_fusion.2
  255.9 0.2 dynamic_update_slice.37
  256.1 5.6 fusion.37
  261.7 2.9 fusion.38
  264.7 3.1 multiply_reduce_fusion.5
  267.7 1.5 exponential_reduce_fusion.5
  269.2 1.3 multiply_reduce_fusion.6
  270.6 1.5 exponential_reduce_fusion.4
  272.1 5.7 subtract_convert_fusion.2
  277.8 0.2 dynamic_update_slice.37
  277.9 5.6 fusion.37
  283.5 0.0 copy-done
  283.5 2.9 fusion.38
  286.5 3.1 multiply_reduce_fusion.5
  289.5 1.5 exponential_reduce_fusion.5
  291.0 1.3 multiply_reduce_fusion.6
  292.4 1.5 exponential_reduce_fusion.4
  293.9 5.7 subtract_convert_fusion.2
  299.6 0.2 dynamic_update_slice.37
  299.7 5.6 fusion.37
  305.4 2.9 fusion.38
  308.3 3.1 multiply_reduce_fusion.5
  311.4 1.5 exponential_reduce_fusion.5
  312.9 1.3 multiply_reduce_fusion.6
  314.2 1.5 exponential_reduce_fusion.4
  315.7 5.7 subtract_convert_fusion.2
  321.4 0.2 dynamic_update_slice.37
  321.6 5.6 fusion.37
  327.2 2.9 fusion.38
  330.1 5.2 all-to-all-start.2
  335.4 2.9 copy.22
  338.2 48.9 %all-to-all-done.2 = f32[32,256,128]{2,1,0:T(8,128)} async-done(((f32[32,256,128]{2,1,0:T(8,128)}), f32[32,256,128]{2,1,0:T(8,128)}, u32[]{:S(2)}, u32[]{:S(2)}) %all-to-all-start.2) | async-done | bytes 4194336 | tf_op jit(solution)/shard_map/all_to_all | solution.py:134
  387.1 10.0 %all-to-all-start.4 = ((bf16[256,32,128]{2,0,1:T(8,128)(2,1)}), bf16[256,32,128]{2,0,1:T(8,128)(2,1)S(1)}, u32[]{:S(2)}, u32[]{:S(2)}) async-start(bf16[256,32,128]{2,0,1:T(8,128)(2,1)} %copy.22), calls=%async_computation.4 | async-start | bytes 4194304 | tf_op jit(solution)/shard_map/all_to_all | solution.py:143
  397.2 2.6 bitcast_reduce_fusion
  399.8 0.2 copy.21
  400.0 26.7 %all-to-all-done.4 = bf16[256,32,128]{2,0,1:T(8,128)(2,1)S(1)} async-done(((bf16[256,32,128]{2,0,1:T(8,128)(2,1)}), bf16[256,32,128]{2,0,1:T(8,128)(2,1)S(1)}, u32[]{:S(2)}, u32[]{:S(2)}) %all-to-all-start.4) | async-done | bytes 2097184 | tf_op jit(solution)/shard_map/all_to_all | solution.py:143
  426.7 1.9 stack.2
  428.7 193.0 %all_to_all.59 = bf16[32,256,1024]{1,2,0:T(8,128)(2,1)S(1)} all-to-all(bf16[32,256,1024]{1,2,0:T(8,128)(2,1)S(1)} %stack.2), channel_id=1, replica_groups=mesh['tp'=4,'dp'=32] {'dp'}, dimensions={0} | all-to-all | bytes 33554432 | tf_op jit(solution)/shard_map/all_to_all | solution.py:147
  621.7 4.5 fusion.19
  626.2 1.0 copy.23
  (21 shorter events, 0.1 us)
Async XLA Ops:
  7.2 112.9 %all-gather.2.cloned.1.call-start = ((), (), s32[]{:S(2)}) async-start(), calls=%async_computation.5 | async-start | bytes 8650752 | tf_op jit(solution)/shard_map/all_gather | solution.py:60
  10.7 31.7 %all-to-all-start = ((bf16[4,256,1024]{1,2,0:T(8,128)(2,1)}), bf16[4,256,1024]{1,2,0:T(8,128)(2,1)S(1)}, u32[]{:S(2)}, u32[]{:S(2)}) async-start(bf16[4,256,1024]{1,2,0:T(8,128)(2,1)} %broadcast_in_dim.29), calls=%async_computation | async-start | bytes 4194304 | tf_op jit(solution)/shard_map/all_to_all | solution.py:13
  42.4 83.4 %copy-start.1 = (bf16[4,256,1024]{1,2,0:T(8,128)(2,1)}, bf16[4,256,1024]{1,2,0:T(8,128)(2,1)S(1)}, u32[]{:S(2)}) copy-start(bf16[4,256,1024]{1,2,0:T(8,128)(2,1)S(1)} %all-to-all-done) | copy-start | bytes 6291460
  130.3 104.0 %all-to-all-start.1 = ((bf16[256,32,384]{2,0,1:T(8,128)(2,1)}), bf16[256,32,384]{2,0,1:T(8,128)(2,1)}, u32[]{:S(2)}, u32[]{:S(2)}) async-start(bf16[256,32,384]{2,0,1:T(8,128)(2,1)} %pad_maximum_fusion), calls=%async_computation.1 | async-start | bytes 12582912 | tf_op jit(solution)/shard_map/all_to_all | solution.py:35
  256.1 5.6 copy-start
  277.9 5.6 copy-start
  299.7 5.6 copy-start
  321.6 5.6 copy-start
  330.1 8.1 %copy-start.3 = (f32[2048]{0:T(1024)}, f32[2048]{0:T(1024)S(1)}, u32[]{:S(2)}) copy-start(f32[2048]{0:T(1024)S(1)} %get-tuple-element.161) | copy-start | bytes 24580
  330.1 5.2 copy-start.2
  330.1 57.0 %all-to-all-start.2 = ((f32[32,256,128]{2,1,0:T(8,128)}), f32[32,256,128]{2,1,0:T(8,128)}, u32[]{:S(2)}, u32[]{:S(2)}) async-start(f32[32,256,128]{2,1,0:T(8,128)} %bitcast.52), calls=%async_computation.2 | async-start | bytes 8388608 | tf_op jit(solution)/shard_map/all_to_all | solution.py:134
  387.1 39.6 %all-to-all-start.4 = ((bf16[256,32,128]{2,0,1:T(8,128)(2,1)}), bf16[256,32,128]{2,0,1:T(8,128)(2,1)S(1)}, u32[]{:S(2)}, u32[]{:S(2)}) async-start(bf16[256,32,128]{2,0,1:T(8,128)(2,1)} %copy.22), calls=%async_computation.4 | async-start | bytes 4194304 | tf_op jit(solution)/shard_map/all_to_all | solution.py:143
Sparse Core Ops, SparseCore 0:
  11.0 108.9 all-gather.1
